TPU v7x, 32 devices: a whole 2x2x4 slice. The times are simulated.
32 devices in a mesh: expert: 8 (over z, x), fsdp: 4 (over y, core).
Axes of the slice: x: 2, y: 2, z: 4, core: 2. Of those that a mesh axis runs over, the one named last changes fastest.
Arguments:
- tokens: bfloat16 [160, 197, 512], P(('expert', 'fsdp')), may hold values from -6 to 6
- ln1_gain: bfloat16 [512], P('fsdp'), may hold values from 0.5 to 1.5
- ln1_bias: bfloat16 [512], P('fsdp'), may hold values from -1.796875 to 1.796875
- w_qkv: bfloat16 [512, 1536], P('fsdp'), may hold values from -0.25 to 0.25
- q_bias: bfloat16 [512], P('fsdp'), may hold values from -1.796875 to 1.796875
- v_bias: bfloat16 [512], P('fsdp'), may hold values from -1.796875 to 1.796875
- w_out: bfloat16 [512, 512], P('fsdp'), may hold values from -1.5 to 1.5
- out_bias: bfloat16 [512], P('fsdp'), may hold values from -1.796875 to 1.796875
- ln2_gain: bfloat16 [512], P('fsdp'), may hold values from 0.5 to 1.5
- ln2_bias: bfloat16 [512], P('fsdp'), may hold values from -1.796875 to 1.796875
- w_router: bfloat16 [512, 8], P('fsdp'), may hold values from -0.1875 to 0.1875
- expert_w1: bfloat16 [8, 512, 2048], P('expert', 'fsdp'), may hold values from -0.25 to 0.25
- expert_b1: bfloat16 [8, 2048], P('expert', 'fsdp'), may hold values from -1.796875 to 1.796875
- expert_w2: bfloat16 [8, 2048, 512], P('expert', 'fsdp'), may hold values from -0.75 to 0.75
- expert_b2: bfloat16 [8, 512], P('expert', 'fsdp'), may hold values from -6 to 6
- route_ids: int32 [31520, 2], P(('expert', 'fsdp')), may hold values from 0 to 7, all different within a row; in each aligned block of 985 rows (0 to 984, 985 to 1969, ...) at most 432 rows name the same one
- clip_threshold: int32 [8], replicated, may hold values from 2 to 4
- grad_output: bfloat16 [160, 197, 512], P(('expert', 'fsdp')), may hold values from -6 to 6
Outputs:
- output: bfloat16 [160, 197, 512], P(('expert', 'fsdp'))
- input_grad: float32 [160, 197, 512], P(('expert', 'fsdp'))
- grad_ln1_gain: float32 [512], P('fsdp')
- grad_ln1_bias: float32 [512], P('fsdp')
- grad_w_qkv: float32 [512, 1536], P('fsdp')
- grad_q_bias: float32 [512], P('fsdp')
- grad_v_bias: float32 [512], P('fsdp')
- grad_w_out: float32 [512, 512], P('fsdp')
- grad_out_bias: float32 [512], P('fsdp')
- grad_ln2_gain: float32 [512], P('fsdp')
- grad_ln2_bias: float32 [512], P('fsdp')
- grad_w_router: float32 [512, 8], P('fsdp')
- grad_expert_w1: float32 [8, 512, 2048], P('expert', 'fsdp')
- grad_expert_b1: float32 [8, 2048], P('expert', 'fsdp')
- grad_expert_w2: float32 [8, 2048, 512], P('expert', 'fsdp')
- grad_expert_b2: float32 [8, 512], P('expert', 'fsdp')
- clipped_qkv: bfloat16 [512, 1536], P('fsdp')
Inputs may be any that keep to these rules, and one draw needn't show every extreme that they name: `route_ids`: each row names 2 different experts; among the 985 rows of one device no expert is named by more than 432 rows, and in some device's rows one expert is named by exactly 432.
All inputs are finite; a program needn't handle non-finite values.
Results may differ from a plain program's by a relative error of at most 0.024.
Values may be sent and summed in bfloat16 or wider, within the bound.
No kernel may reach another device: no remote copies, remote signals or barrier semaphores. Data moves between devices by JAX's collectives and lax.ppermute only.
A program may use at most 256 MiB of HBM per device.

v0:
```python
import jax
import jax.numpy as jnp
from jax import lax
from jax.sharding import PartitionSpec as P

HEADS = 8
norm_eps = 1e-06
highest = lax.Precision.HIGHEST


def layer_norm(matrix, norm_gain, norm_shift):
    centred = matrix - jnp.mean(matrix, axis=1, keepdims=True)
    inverse = lax.rsqrt(jnp.mean(centred * centred, axis=1, keepdims=True) + norm_eps)
    normed = centred * inverse
    return (normed * norm_gain + norm_shift, normed, inverse)


def norm_backward(upstream, norm_gain, normed, inverse):
    scaled = upstream * norm_gain
    spread = (
        scaled
        - jnp.mean(scaled, axis=1, keepdims=True)
        - normed * jnp.mean(scaled * normed, axis=1, keepdims=True)
    )
    return (spread * inverse, jnp.sum(upstream * normed, axis=0), jnp.sum(upstream, axis=0))


def gelu_exact(values):
    return jax.nn.gelu(values, approximate=False)


def shards(
    tokens,
    ln1_gain,
    ln1_bias,
    w_qkv,
    q_bias,
    v_bias,
    w_out,
    out_bias,
    ln2_gain,
    ln2_bias,
    w_router,
    expert_w1,
    expert_b1,
    expert_w2,
    expert_b2,
    route_ids,
    clip_threshold,
    grad_output,
):
    gathered = (
        lax.all_gather(ln1_gain, "fsdp", axis=0, tiled=True),
        lax.all_gather(ln1_bias, "fsdp", axis=0, tiled=True),
        lax.all_gather(w_qkv, "fsdp", axis=0, tiled=True),
        lax.all_gather(q_bias, "fsdp", axis=0, tiled=True),
        lax.all_gather(v_bias, "fsdp", axis=0, tiled=True),
        lax.all_gather(w_out, "fsdp", axis=0, tiled=True),
        lax.all_gather(out_bias, "fsdp", axis=0, tiled=True),
        lax.all_gather(ln2_gain, "fsdp", axis=0, tiled=True),
        lax.all_gather(ln2_bias, "fsdp", axis=0, tiled=True),
        lax.all_gather(w_router, "fsdp", axis=0, tiled=True),
        lax.all_gather(expert_w1, "fsdp", axis=1, tiled=True),
        lax.all_gather(expert_b1, "fsdp", axis=1, tiled=True),
        lax.all_gather(expert_w2, "fsdp", axis=1, tiled=True),
        lax.all_gather(expert_b2, "fsdp", axis=1, tiled=True),
    )
    gain_one = gathered[0].astype(jnp.float32)
    shift_one = gathered[1].astype(jnp.float32)
    qkv_weight = gathered[2]
    query_bias = gathered[3].astype(jnp.float32)
    value_bias = gathered[4].astype(jnp.float32)
    out_weight = gathered[5]
    out_shift = gathered[6].astype(jnp.float32)
    gain_two = gathered[7].astype(jnp.float32)
    shift_two = gathered[8].astype(jnp.float32)
    router_weight = gathered[9].astype(jnp.float32)
    first_weight = gathered[10][0]
    first_bias = gathered[11][0].astype(jnp.float32)
    second_weight = gathered[12][0]
    second_bias = gathered[13][0].astype(jnp.float32)
    image_count, sequence, feature_width = tokens.shape
    token_count = image_count * sequence
    head_count = HEADS
    head_size = feature_width // head_count
    score_scale = head_size ** (-0.5)
    route_top = route_ids.shape[1]
    expert_total = router_weight.shape[1]
    capacity = (7 * token_count // (2 * expert_total) + 7) // 8 * 8
    head_shape = (image_count, sequence, head_count, head_size)
    residual = tokens.astype(jnp.float32).reshape(token_count, feature_width)
    normed_in, hat_one, inverse_one = layer_norm(residual, gain_one, shift_one)
    normed_low = normed_in.astype(jnp.bfloat16)
    projected = jnp.dot(normed_low, qkv_weight, preferred_element_type=jnp.float32)
    queries = (projected[:, :feature_width] + query_bias).astype(jnp.bfloat16).reshape(head_shape)
    key_rows = (
        projected[:, feature_width : 2 * feature_width].astype(jnp.bfloat16).reshape(head_shape)
    )
    value_rows = (
        (projected[:, 2 * feature_width :] + value_bias).astype(jnp.bfloat16).reshape(head_shape)
    )
    scores = (
        jnp.einsum("bqhd,bkhd->bhqk", queries, key_rows, preferred_element_type=jnp.float32)
        * score_scale
    )
    head_peak = jnp.max(scores, axis=(0, 2, 3))
    row_top = jnp.max(scores, axis=3, keepdims=True)
    log_total = row_top + jnp.log(jnp.sum(jnp.exp(scores - row_top), axis=3, keepdims=True))
    attn_low = jnp.exp(scores - log_total).astype(jnp.bfloat16)
    mixed_rows = jnp.einsum(
        "bhqk,bkhd->bqhd", attn_low, value_rows, preferred_element_type=jnp.float32
    )
    mixed_low = mixed_rows.astype(jnp.bfloat16).reshape(token_count, feature_width)
    hidden = (
        residual + jnp.dot(mixed_low, out_weight, preferred_element_type=jnp.float32) + out_shift
    )
    normed_mid, hat_two, inverse_two = layer_norm(hidden, gain_two, shift_two)
    route_prob = jax.nn.softmax(jnp.dot(normed_mid, router_weight, precision=highest), axis=1)
    picked = (
        route_ids[:, :, None] == lax.broadcasted_iota(jnp.int32, (1, 1, expert_total), 2)
    ).astype(jnp.int32)
    picked_float = picked.astype(jnp.float32)
    gate_values = jnp.sum(picked_float * route_prob[:, None, :], axis=2)
    picked_flat = picked.reshape(token_count * route_top, expert_total)
    slot_rank = jnp.sum(
        (jnp.cumsum(picked_flat, axis=0, dtype=jnp.int32) - picked_flat) * picked_flat,
        axis=1,
        dtype=jnp.int32,
    )
    slot_index = route_ids.reshape(-1) * capacity + slot_rank
    mid_low = normed_mid.astype(jnp.bfloat16)
    slot_rows = jnp.broadcast_to(
        mid_low[:, None, :], (token_count, route_top, feature_width)
    ).reshape(token_count * route_top, feature_width)
    outgoing = (
        jnp.zeros((expert_total * capacity, feature_width), jnp.bfloat16)
        .at[slot_index]
        .set(slot_rows)
        .reshape(expert_total, capacity, feature_width)
    )
    arrived = lax.all_to_all(outgoing, "expert", split_axis=0, concat_axis=0, tiled=True)
    flat_in = arrived.reshape(-1, feature_width)
    activation = gelu_exact(
        jnp.dot(flat_in, first_weight, preferred_element_type=jnp.float32) + first_bias
    ).astype(jnp.bfloat16)
    result = (
        jnp.dot(activation, second_weight, preferred_element_type=jnp.float32) + second_bias
    ).astype(jnp.bfloat16)
    produced = result.reshape(arrived.shape)
    returned = lax.all_to_all(produced, "expert", split_axis=0, concat_axis=0, tiled=True)
    slot_out = (
        returned.reshape(expert_total * capacity, feature_width)[slot_index]
        .astype(jnp.float32)
        .reshape(token_count, route_top, feature_width)
    )
    output = (
        (hidden + jnp.sum(gate_values[:, :, None] * slot_out, axis=1))
        .astype(jnp.bfloat16)
        .reshape(tokens.shape)
    )
    upstream = grad_output.astype(jnp.float32).reshape(token_count, feature_width)
    gate_grad = jnp.sum(slot_out * upstream[:, None, :], axis=2)
    slot_grad = (
        (gate_values[:, :, None] * upstream[:, None, :])
        .astype(jnp.bfloat16)
        .reshape(token_count * route_top, feature_width)
    )
    grad_buffer = (
        jnp.zeros((expert_total * capacity, feature_width), jnp.bfloat16)
        .at[slot_index]
        .set(slot_grad)
        .reshape(expert_total, capacity, feature_width)
    )
    grad_arrived = lax.all_to_all(grad_buffer, "expert", split_axis=0, concat_axis=0, tiled=True)
    flat_rows = arrived.reshape(-1, feature_width)
    flat_grad = grad_arrived.reshape(-1, feature_width)
    activation, gelu_back = jax.vjp(
        gelu_exact,
        jnp.dot(flat_rows, first_weight, preferred_element_type=jnp.float32) + first_bias,
    )
    act_low = activation.astype(jnp.bfloat16)
    grad_second = jnp.einsum("rh,rd->hd", act_low, flat_grad, preferred_element_type=jnp.float32)
    grad_second_bias = jnp.sum(flat_grad, axis=0, dtype=jnp.float32)
    act_grad = jnp.einsum("rd,hd->rh", flat_grad, second_weight, preferred_element_type=jnp.float32)
    pre_grad = gelu_back(act_grad)[0].astype(jnp.bfloat16)
    grad_first = jnp.einsum("rd,rh->dh", flat_rows, pre_grad, preferred_element_type=jnp.float32)
    grad_first_bias = jnp.sum(pre_grad, axis=0, dtype=jnp.float32)
    row_grad = (
        jnp.einsum("rh,dh->rd", pre_grad, first_weight, preferred_element_type=jnp.float32)
        .astype(jnp.bfloat16)
        .reshape(grad_arrived.shape)
    )
    row_back = lax.all_to_all(row_grad, "expert", split_axis=0, concat_axis=0, tiled=True)
    slot_back = (
        row_back.reshape(expert_total * capacity, feature_width)[slot_index]
        .astype(jnp.float32)
        .reshape(token_count, route_top, feature_width)
    )
    prob_grad = jnp.sum(picked_float * gate_grad[:, :, None], axis=1)
    logit_grad = route_prob * (prob_grad - jnp.sum(route_prob * prob_grad, axis=1, keepdims=True))
    mid_grad = jnp.sum(slot_back, axis=1) + jnp.einsum(
        "re,de->rd", logit_grad, router_weight, precision=highest
    )
    grad_router = jnp.einsum("rd,re->de", normed_mid, logit_grad, precision=highest)
    norm_part, grad_gain_two, grad_shift_two = norm_backward(
        mid_grad, gain_two, hat_two, inverse_two
    )
    hidden_grad = upstream + norm_part
    branch_low = hidden_grad.astype(jnp.bfloat16)
    grad_out_weight = jnp.einsum(
        "rd,re->de", mixed_low, branch_low, preferred_element_type=jnp.float32
    )
    grad_out_shift = jnp.sum(branch_low, axis=0, dtype=jnp.float32)
    mixed_grad = (
        jnp.einsum("re,de->rd", branch_low, out_weight, preferred_element_type=jnp.float32)
        .astype(jnp.bfloat16)
        .reshape(head_shape)
    )
    score_again = (
        jnp.einsum("bqhd,bkhd->bhqk", queries, key_rows, preferred_element_type=jnp.float32)
        * score_scale
    )
    attn_prob = jnp.exp(score_again - log_total)
    value_grad = jnp.einsum(
        "bhqk,bqhd->bkhd",
        attn_prob.astype(jnp.bfloat16),
        mixed_grad,
        preferred_element_type=jnp.float32,
    ).astype(jnp.bfloat16)
    weight_grad = jnp.einsum(
        "bqhd,bkhd->bhqk", mixed_grad, value_rows, preferred_element_type=jnp.float32
    )
    score_grad = (
        attn_prob * (weight_grad - jnp.sum(attn_prob * weight_grad, axis=3, keepdims=True))
    ).astype(jnp.bfloat16)
    query_grad = (
        jnp.einsum("bhqk,bkhd->bqhd", score_grad, key_rows, preferred_element_type=jnp.float32)
        * score_scale
    ).astype(jnp.bfloat16)
    key_grad = (
        jnp.einsum("bhqk,bqhd->bkhd", score_grad, queries, preferred_element_type=jnp.float32)
        * score_scale
    ).astype(jnp.bfloat16)
    qkv_grad = jnp.concatenate(
        [
            query_grad.reshape(token_count, feature_width),
            key_grad.reshape(token_count, feature_width),
            value_grad.reshape(token_count, feature_width),
        ],
        axis=1,
    )
    grad_qkv = jnp.einsum("rd,re->de", normed_low, qkv_grad, preferred_element_type=jnp.float32)
    grad_query_bias = jnp.sum(qkv_grad[:, :feature_width], axis=0, dtype=jnp.float32)
    grad_value_bias = jnp.sum(qkv_grad[:, 2 * feature_width :], axis=0, dtype=jnp.float32)
    in_grad = jnp.einsum("re,de->rd", qkv_grad, qkv_weight, preferred_element_type=jnp.float32)
    input_part, grad_gain_one, grad_shift_one = norm_backward(
        in_grad, gain_one, hat_one, inverse_one
    )
    input_grad = (hidden_grad + input_part).reshape(tokens.shape)
    shares = (
        lax.psum_scatter(
            grad_gain_one.astype(jnp.bfloat16), "fsdp", scatter_dimension=0, tiled=True
        ).astype(jnp.float32),
        lax.psum_scatter(
            grad_shift_one.astype(jnp.bfloat16), "fsdp", scatter_dimension=0, tiled=True
        ).astype(jnp.float32),
        lax.psum_scatter(
            grad_qkv.astype(jnp.bfloat16), "fsdp", scatter_dimension=0, tiled=True
        ).astype(jnp.float32),
        lax.psum_scatter(
            grad_query_bias.astype(jnp.bfloat16), "fsdp", scatter_dimension=0, tiled=True
        ).astype(jnp.float32),
        lax.psum_scatter(
            grad_value_bias.astype(jnp.bfloat16), "fsdp", scatter_dimension=0, tiled=True
        ).astype(jnp.float32),
        lax.psum_scatter(
            grad_out_weight.astype(jnp.bfloat16), "fsdp", scatter_dimension=0, tiled=True
        ).astype(jnp.float32),
        lax.psum_scatter(
            grad_out_shift.astype(jnp.bfloat16), "fsdp", scatter_dimension=0, tiled=True
        ).astype(jnp.float32),
        lax.psum_scatter(
            grad_gain_two.astype(jnp.bfloat16), "fsdp", scatter_dimension=0, tiled=True
        ).astype(jnp.float32),
        lax.psum_scatter(
            grad_shift_two.astype(jnp.bfloat16), "fsdp", scatter_dimension=0, tiled=True
        ).astype(jnp.float32),
        lax.psum_scatter(
            grad_router.astype(jnp.bfloat16), "fsdp", scatter_dimension=0, tiled=True
        ).astype(jnp.float32),
    )
    summed = (
        lax.psum(shares[0].astype(jnp.bfloat16), "expert").astype(jnp.float32),
        lax.psum(shares[1].astype(jnp.bfloat16), "expert").astype(jnp.float32),
        lax.psum(shares[2].astype(jnp.bfloat16), "expert").astype(jnp.float32),
        lax.psum(shares[3].astype(jnp.bfloat16), "expert").astype(jnp.float32),
        lax.psum(shares[4].astype(jnp.bfloat16), "expert").astype(jnp.float32),
        lax.psum(shares[5].astype(jnp.bfloat16), "expert").astype(jnp.float32),
        lax.psum(shares[6].astype(jnp.bfloat16), "expert").astype(jnp.float32),
        lax.psum(shares[7].astype(jnp.bfloat16), "expert").astype(jnp.float32),
        lax.psum(shares[8].astype(jnp.bfloat16), "expert").astype(jnp.float32),
        lax.psum(shares[9].astype(jnp.bfloat16), "expert").astype(jnp.float32),
    )
    expert_summed = (
        lax.psum_scatter(
            grad_first[None].astype(jnp.bfloat16), "fsdp", scatter_dimension=1, tiled=True
        ).astype(jnp.float32),
        lax.psum_scatter(
            grad_first_bias[None].astype(jnp.bfloat16), "fsdp", scatter_dimension=1, tiled=True
        ).astype(jnp.float32),
        lax.psum_scatter(
            grad_second[None].astype(jnp.bfloat16), "fsdp", scatter_dimension=1, tiled=True
        ).astype(jnp.float32),
        lax.psum_scatter(
            grad_second_bias[None].astype(jnp.bfloat16), "fsdp", scatter_dimension=1, tiled=True
        ).astype(jnp.float32),
    )
    peak_logit = lax.pmax(head_peak, ("expert", "fsdp"))
    limit_value = clip_threshold.astype(jnp.float32)
    root_factor = jnp.sqrt(limit_value / jnp.maximum(peak_logit, limit_value))
    column_scale = jnp.concatenate(
        [
            jnp.repeat(root_factor, head_size),
            jnp.repeat(root_factor, head_size),
            jnp.ones((feature_width,), jnp.float32),
        ]
    )
    clipped_qkv = (w_qkv.astype(jnp.float32) * column_scale).astype(jnp.bfloat16)
    return (
        output,
        input_grad,
        summed[0],
        summed[1],
        summed[2],
        summed[3],
        summed[4],
        summed[5],
        summed[6],
        summed[7],
        summed[8],
        summed[9],
        expert_summed[0],
        expert_summed[1],
        expert_summed[2],
        expert_summed[3],
        clipped_qkv,
    )


def solution(mesh):
    placed = (
        P(("expert", "fsdp"), None, None),
        P("fsdp"),
        P("fsdp"),
        P("fsdp", None),
        P("fsdp"),
        P("fsdp"),
        P("fsdp", None),
        P("fsdp"),
        P("fsdp"),
        P("fsdp"),
        P("fsdp", None),
        P("expert", "fsdp", None),
        P("expert", "fsdp"),
        P("expert", "fsdp", None),
        P("expert", "fsdp"),
        P(("expert", "fsdp"), None),
        P(),
        P(("expert", "fsdp"), None, None),
    )
    return jax.shard_map(
        shards,
        mesh=mesh,
        in_specs=placed,
        out_specs=(
            P(("expert", "fsdp"), None, None),
            P(("expert", "fsdp"), None, None),
            P("fsdp"),
            P("fsdp"),
            P("fsdp", None),
            P("fsdp"),
            P("fsdp"),
            P("fsdp", None),
            P("fsdp"),
            P("fsdp"),
            P("fsdp"),
            P("fsdp", None),
            P("expert", "fsdp", None),
            P("expert", "fsdp"),
            P("expert", "fsdp", None),
            P("expert", "fsdp"),
            P("fsdp", None),
        ),
        check_vma=False,
    )
```

profile of v0, /device:TPU:0, one launch (start us, length us, event | category | flops | bytes accessed | tf_op | source)
XLA Modules:
  0.0 718.8 jit_solution(18381751544721613083)
XLA Ops:
  52.3 7.9 %all_gather.47 = bf16[512,512]{1,0:T(8,128)(2,1)} all-gather(bf16[128,512]{1,0:T(8,128)(2,1)S(1)} %copy-done.46), channel_id=1, replica_groups=mesh['expert'=8,'fsdp'=4] {'fsdp'}, dimensions={0}, use_global_device_ids=true | all-gather | bytes 655360 | tf_op jit(solution)/shard_map/all_gather | solution.py:58
  108.3 13.3 %scatter_custom_fusion = bf16[3456,512]{1,0:T(8,128)(2,1)} fusion(s32[1970]{0:T(1024)S(1)} %bitcast.131, bf16[1970,512]{1,0:T(8,128)(2,1)} %reshape.330, bf16[]{:T(256)} %constant.17.clone.1), kind=kCustom, calls=%fused_computation.69 | custom fusion | bytes 3539456 | tf_op jit(solution)/shard_map/scatter | solution.py:138
  121.6 6.0 all-to-all-start
  135.5 6.1 mul.252
  161.2 18.5 %scatter_custom_fusion.1 = bf16[3456,512]{1,0:T(8,128)(2,1)} fusion(s32[1970]{0:T(1024)S(1)} %bitcast.132, f32[1970,512]{1,0:T(8,128)} %mul.252, f32[1970]{0:T(1024)S(1)} %mul.249, bf16[]{:T(256)} %constant.17.clone.1), kind=kCustom, calls=%fused_computation.63 | custom fusion | flops 2017280 | bytes 7581698 | tf_op jit(solution)/shard_map/scatter | solution.py:171
  179.8 27.6 %all-to-all-done = bf16[8,432,512]{2,1,0:T(8,128)(2,1)} async-done(((bf16[8,432,512]{2,1,0:T(8,128)(2,1)}), bf16[8,432,512]{2,1,0:T(8,128)(2,1)}, u32[]{:S(2)}, u32[]{:S(2)}) %all-to-all-start) | async-done | bytes 3538976 | tf_op jit(solution)/shard_map/all_to_all | solution.py:141
  212.0 70.8 %multiply_convert_fusion = (bf16[3456,2048]{1,0:T(8,128)(2,1)}, f32[3456,2048]{1,0:T(8,128)}, f32[3456,2048]{1,0:T(8,128)}) fusion(f32[2048]{0:T(1024)S(1)} %bitcast.142, bf16[3456,512]{1,0:T(8,128)(2,1)} %bitcast.19, bf16[1,512,2048]{2,1,0:T(8,128)(2,1)} %all-gather.13.cloned.1.call-done), kind=kOutput, calls=%fused_computation.7 | convolution fusion | flops 7714897920 | bytes 76423168 | tf_op jit(solution)/shard_map/dot_general | solution.py:144
  282.8 12.5 %add_convert_fusion.1 = bf16[3456,512]{1,0:T(8,128)(2,1)} fusion(bf16[3456,2048]{1,0:T(8,128)(2,1)} %get-tuple-element.48, f32[512]{0:T(512)S(1)} %bitcast.144, bf16[1,2048,512]{2,1,0:T(8,128)(2,1)} %all-gather.15.cloned.1.call-done), kind=kOutput, calls=%fused_computation.25 | convolution fusion | flops 7251296256 | bytes 19793920 | tf_op jit(solution)/shard_map/dot_general | solution.py:147
  305.0 31.9 %fusion.50 = (bf16[2048]{0:T(1024)(128)(2,1)S(1)}, bf16[3456,2048]{1,0:T(8,128)(2,1)}) fusion(f32[3456,2048]{1,0:T(8,128)} %get-tuple-element.49, bf16[3456,512]{1,0:T(8,128)(2,1)} %bitcast.27, bf16[1,2048,512]{2,1,0:T(8,128)(2,1)} %all-gather.15.cloned.1.call-done, f32[3456,2048]{1,0:T(8,128)} %get-tuple-element.57, f32[2048]{0:T(1024)S(1)} %bitcast.143), kind=kOutput, calls=%fused_computation.138 | convolution fusion | flops 7361001472 | bytes 76427264 | tf_op jit(solution)/shard_map/rd,hd->rh/dot_general | solution.py:184
  338.1 12.6 %convolution_convert_fusion = bf16[3456,512]{1,0:T(8,128)(2,1)} fusion(bf16[3456,2048]{1,0:T(8,128)(2,1)} %get-tuple-element.68, bf16[1,512,2048]{2,1,0:T(8,128)(2,1)} %all-gather.13.cloned.1.call-done), kind=kOutput, calls=%fused_computation.28 | convolution fusion | flops 7249526784 | bytes 19791872 | tf_op jit(solution)/shard_map/rh,dh->rd/dot_general | solution.py:189
  350.7 28.8 %all-to-all-done.1 = bf16[8,432,512]{2,1,0:T(8,128)(2,1)S(1)} async-done(((bf16[8,432,512]{2,1,0:T(8,128)(2,1)}), bf16[8,432,512]{2,1,0:T(8,128)(2,1)S(1)}, u32[]{:S(2)}, u32[]{:S(2)}) %all-to-all-start.1) | async-done | bytes 3538976 | tf_op jit(solution)/shard_map/all_to_all | solution.py:150
  384.1 13.0 %fusion.7 = bf16[1,2048,512]{2,1,0:T(8,128)(2,1)} fusion(bf16[3456,2048]{1,0:T(8,128)(2,1)} %get-tuple-element.48, bf16[3456,512]{1,0:T(8,128)(2,1)} %bitcast.27), kind=kOutput, calls=%fused_computation.36 | convolution fusion | flops 7248805888 | bytes 19791872 | tf_op jit(solution)/shard_map/rh,rd->hd/dot_general | solution.py:182
  397.7 13.0 %fusion.8 = bf16[1,512,2048]{2,1,0:T(8,128)(2,1)} fusion(bf16[3456,512]{1,0:T(8,128)(2,1)} %bitcast.19, bf16[3456,2048]{1,0:T(8,128)(2,1)} %get-tuple-element.68), kind=kOutput, calls=%fused_computation.37 | convolution fusion | flops 7248805888 | bytes 19791872 | tf_op jit(solution)/shard_map/rd,rh->dh/dot_general | solution.py:186
  410.7 9.1 %gather_fusion = bf16[1970,512]{1,0:T(8,128)(2,1)} fusion(bf16[3456,512]{1,0:T(8,128)(2,1)S(1)} %bitcast.112, s32[2048]{0:T(1024)S(1)} %pad_clamp_fusion), kind=kCustom, calls=%fused_computation | custom fusion | bytes 4042440 | tf_op jit(solution)/shard_map/gather | solution.py:152
  425.5 13.6 %multiply_reduce_fusion.3 = (f32[985,2]{1,0:T(8,128)S(1)}, f32[985,512]{1,0:T(8,128)}) fusion(f32[985,2,512]{2,1,0:T(2,128)} %reshape.306, f32[985,512]{1,0:T(8,128)S(1)} %copy-done.7, f32[985,2]{1,0:T(8,128)S(1)} %copy-done.23), kind=kLoop, calls=%fused_computation.31 | loop fusion | flops 3528270 | bytes 8084880 | tf_op jit(solution)/shard_map/reduce_sum | solution.py:162
  439.4 23.3 %all-to-all-done.3 = bf16[8,432,512]{2,1,0:T(8,128)(2,1)} async-done(((bf16[8,432,512]{2,1,0:T(8,128)(2,1)}), bf16[8,432,512]{2,1,0:T(8,128)(2,1)}, u32[]{:S(2)}, u32[]{:S(2)}) %all-to-all-start.3) | async-done | bytes 3538976 | tf_op jit(solution)/shard_map/all_to_all | solution.py:193
  462.7 10.4 %gather_fusion.1 = bf16[1970,512]{1,0:T(8,128)(2,1)S(1)} fusion(bf16[3456,512]{1,0:T(8,128)(2,1)} %bitcast.29, s32[2048]{0:T(1024)S(1)} %pad_clamp_fusion), kind=kCustom, calls=%fused_computation.1 | custom fusion | bytes 4042440 | tf_op jit(solution)/shard_map/gather | solution.py:195
  477.8 8.4 %reduce_sum.274 = f32[985,512]{1,0:T(8,128)} reduce(f32[985,2,512]{2,1,0:T(2,128)} %reshape.309, f32[]{:T(128)} %constant.40.clone.1), dimensions={1}, to_apply=%region_15.16 | reduce | flops 504320 | bytes 6051844 | tf_op jit(solution)/shard_map/reduce_sum | solution.py:201
  503.6 6.7 multiply_reduce_fusion.1
  563.9 38.0 %pmax.7 = f32[8]{0:T(128)S(1)} all-reduce(f32[8]{0:T(128)S(1)} %get-tuple-element.17), channel_id=1, replica_groups=mesh['expert'=8,'fsdp'=4] {'expert','fsdp'}, use_global_device_ids=true, to_apply=%region_58.59 | all-reduce | flops 8 | bytes 64 | tf_op jit(solution)/shard_map/pmax | solution.py:318
  604.4 6.5 multiply_reduce_fusion.7
  615.1 6.4 all-reduce.10
  632.5 21.7 %all-reduce.8 = (bf16[128]{0:T(256)(128)(2,1)S(1)}, bf16[128]{0:T(256)(128)(2,1)S(1)}, bf16[128]{0:T(256)(128)(2,1)S(1)}, bf16[128]{0:T(256)(128)(2,1)S(1)}, bf1...) all-reduce(bf16[128]{0:T(256)(128)(2,1)S(1)} %dynamic-slice.1, ...), channel_id=1, replica_groups=mesh['expert'=8,'fsdp'=4] {'expert'}, use_global_device_ids=true, to_apply=%region_26.27 | all-reduce | flops 1920 | bytes 7680 | tf_op jit(solution)/shard_map/psum | solution.py:293
  658.4 49.8 %all-reduce.13.cloned.1.call-done = (bf16[128,1536]{1,0:T(8,128)(2,1)}, bf16[128,512]{1,0:T(8,128)(2,1)}) async-done(((bf16[128,1536]{1,0:T(8,128)(2,1)}, bf16[128,512]{1,0:T(8,128)(2,1)}), (bf16[128,1536]{1,0:T(8,128)(2,1)}, bf16[128,512]{1,0:T(8,128)(2,1)})) %all-reduce.13.cloned.1.call-update) | async-done | bytes 524304 | tf_op jit(solution)/shard_map/psum | solution.py:295
  (334 shorter events, 246.7 us)
Async XLA Ops:
  7.3 53.0 %all-gather.11.cloned.1.call-start = ((), (), s32[]{:S(2)}) async-start(), calls=%async_computation.11 | async-start | bytes 1966080 | tf_op jit(solution)/shard_map/all_gather | solution.py:55
  11.0 52.5 %copy-start.4 = (f32[985,512]{1,0:T(8,128)}, f32[985,512]{1,0:T(8,128)S(1)}, u32[]{:S(2)}) copy-start(f32[985,512]{1,0:T(8,128)S(1)} %reshape.278) | copy-start | bytes 6051844
  11.1 52.4 %copy-start.40 = (f32[985]{0:T(1024)}, f32[985]{0:T(1024)S(1)}, u32[]{:S(2)}) copy-start(f32[985]{0:T(1024)S(1)} %div.38) | copy-start | bytes 11824
  43.3 114.8 %copy-start.51 = (f32[4,1,128]{2,1,0:T(1,128)}, f32[4,1,128]{2,1,0:T(1,128)S(1)}, u32[]{:S(2)}) copy-start(f32[4,1,128]{2,1,0:T(1,128)S(1)} %convert_element_type.339) | copy-start | bytes 6148
  48.3 109.7 %copy-start.61 = (f32[4,1,128]{2,1,0:T(1,128)}, f32[4,1,128]{2,1,0:T(1,128)S(1)}, u32[]{:S(2)}) copy-start(f32[4,1,128]{2,1,0:T(1,128)S(1)} %convert_element_type.340) | copy-start | bytes 6148
  60.2 101.0 %copy-start.59 = (s32[1970,1]{0,1:T(1,128)}, s32[1970,1]{0,1:T(1,128)S(1)}, u32[]{:S(2)}) copy-start(s32[1970,1]{0,1:T(1,128)S(1)} %compare_select_fusion) | copy-start | bytes 23644
  99.6 58.5 %copy-start.1 = (f32[985,512]{1,0:T(8,128)}, f32[985,512]{1,0:T(8,128)S(1)}, u32[]{:S(2)}) copy-start(f32[985,512]{1,0:T(8,128)S(1)} %get-tuple-element.56) | copy-start | bytes 6051844
  99.6 58.5 %copy-start.36 = (f32[985]{0:T(1024)}, f32[985]{0:T(1024)S(1)}, u32[]{:S(2)}) copy-start(f32[985]{0:T(1024)S(1)} %broadcast_multiply_fusion.6) | copy-start | bytes 11824
  100.0 58.0 %copy-start.38 = (f32[985]{0:T(1024)}, f32[985]{0:T(1024)S(1)}, u32[]{:S(2)}) copy-start(f32[985]{0:T(1024)S(1)} %add_rsqrt_fusion.1) | copy-start | bytes 11824
  121.6 85.7 %all-to-all-start = ((bf16[8,432,512]{2,1,0:T(8,128)(2,1)}), bf16[8,432,512]{2,1,0:T(8,128)(2,1)}, u32[]{:S(2)}, u32[]{:S(2)}) async-start(bf16[8,432,512]{2,1,0:T(8,128)(2,1)} %bitcast.113), calls=%async_computation | async-start | bytes 7077888 | tf_op jit(solution)/shard_map/all_to_all | solution.py:141
  127.6 84.4 %all-gather.13.cloned.1.call-start = ((), (), s32[]{:S(2)}) async-start(), calls=%async_computation.12 | async-start | bytes 2621440 | tf_op jit(solution)/shard_map/all_gather | solution.py:63
  128.3 154.5 %all-gather.15.cloned.1.call-start = ((), (), s32[]{:S(2)}) async-start(), calls=%async_computation.13 | async-start | bytes 2621440 | tf_op jit(solution)/shard_map/all_gather | solution.py:65
  207.3 88.1 %all-to-all-start.2 = ((bf16[8,432,512]{2,1,0:T(8,128)(2,1)}), bf16[8,432,512]{2,1,0:T(8,128)(2,1)}, u32[]{:S(2)}, u32[]{:S(2)}) async-start(bf16[8,432,512]{2,1,0:T(8,128)(2,1)} %bitcast.26), calls=%async_computation.2 | async-start | bytes 7077888 | tf_op jit(solution)/shard_map/all_to_all | solution.py:174
  212.0 70.8 %copy-start.65 = (f32[1,512]{1,0:T(1,128)S(1)}, f32[1,512]{1,0:T(1,128)}, u32[]{:S(2)}) copy-start(f32[1,512]{1,0:T(1,128)} %add.210) | copy-start | bytes 6148
  295.4 84.2 %all-to-all-start.1 = ((bf16[8,432,512]{2,1,0:T(8,128)(2,1)}), bf16[8,432,512]{2,1,0:T(8,128)(2,1)S(1)}, u32[]{:S(2)}, u32[]{:S(2)}) async-start(bf16[8,432,512]{2,1,0:T(8,128)(2,1)} %bitcast.115), calls=%async_computation.1 | async-start | bytes 7077888 | tf_op jit(solution)/shard_map/all_to_all | solution.py:150
  301.4 255.3 %reduce-scatter.26.cloned.1.call-start = ((), (), s32[]{:S(2)}) async-start(), calls=%async_computation.20 | async-start | bytes 163840
  304.8 253.3 %reduce-scatter.24.cloned.1.call-start = ((), (), s32[]{:S(2)}) async-start(), calls=%async_computation.19 | async-start | bytes 655360
  379.6 83.1 %all-to-all-start.3 = ((bf16[8,432,512]{2,1,0:T(8,128)(2,1)}), bf16[8,432,512]{2,1,0:T(8,128)(2,1)}, u32[]{:S(2)}, u32[]{:S(2)}) async-start(bf16[8,432,512]{2,1,0:T(8,128)(2,1)} %bitcast.114), calls=%async_computation.3 | async-start | bytes 7077888 | tf_op jit(solution)/shard_map/all_to_all | solution.py:193
  384.1 175.5 %reduce-scatter.20.cloned.1.call-start = ((), (), s32[]{:S(2)}) async-start(), calls=%async_computation.17 | async-start | bytes 2621440 | tf_op jit(solution)/shard_map/reduce_scatter | solution.py:311
  397.2 164.6 %reduce-scatter.18.cloned.1.call-start = ((), (), s32[]{:S(2)}) async-start(), calls=%async_computation.16 | async-start | bytes 2621440 | tf_op jit(solution)/shard_map/reduce_scatter | solution.py:305
  410.7 204.2 %reduce-scatter.16.cloned.1.call-start = ((), (), s32[]{:S(2)}) async-start(), calls=%async_computation.15 | async-start | bytes 655360 | tf_op jit(solution)/shard_map/reduce_scatter | solution.py:276
  520.5 94.3 %reduce-scatter.14.cloned.1.call-start = ((), (), s32[]{:S(2)}) async-start(), calls=%async_computation.14 | async-start | bytes 1966080 | tf_op jit(solution)/shard_map/reduce_scatter | solution.py:267
  555.3 76.4 %reduce-scatter.22.cloned.1.call-start = ((), (), s32[]{:S(2)}) async-start(), calls=%async_computation.18 | async-start | bytes 163840
  610.9 97.3 %all-reduce.13.cloned.1.call-start = ((), (), s32[]{:S(2)}) async-start(), calls=%async_computation.21 | async-start | bytes 1048576 | tf_op jit(solution)/shard_map/psum | solution.py:295
  (69 other events, 825.2 us)
Sparse Core Ops, SparseCore 0:
  9.7 22.3 all-gather.10
  130.0 24.0 all-gather.12
  155.6 22.5 all-gather.14
  304.9 21.0 reduce-scatter.25
  338.2 23.0 reduce-scatter.23
  397.3 32.7 reduce-scatter.19
  432.8 31.4 reduce-scatter.17
  520.6 20.7 reduce-scatter.15
  555.4 27.4 reduce-scatter.13
  611.0 20.5 reduce-scatter.21
  635.5 72.6 all-reduce.12
where the time goes:
time: 726 us; the launch traced here: 719 us
  matrix products  204 us (28%)
  local copies, waits for them, and re-layouts  138 us (19%)
  waiting for transfers between devices  136 us (19%)
  blocking collectives  126 us (17%)
  other arithmetic  76 us (10%)
  starting transfers between devices  22.2 us (3%)
  between operations  16.1 us (2%)
    dot_general x1, matrix products, shards(): jnp.dot(flat_in, first_weight, preferred_element_type=jnp.float32)  70.8 us
    psum x1, waiting for transfers between devices, shards(): lax.psum(shares[2].astype(jnp.bfloat16), 'expert').astype(jnp.float32)  49.8 us
    pmax x1, blocking collectives, shards(): peak_logit = lax.pmax(head_peak, ('expert', 'fsdp'))  38 us
    dot_general x1, matrix products, shards(): jnp.einsum('rd,hd->rh', flat_grad, second_weight, preferred_element_type=...  31.9 us
    all_to_all x1, waiting for transfers between devices, shards(): lax.all_to_all(produced, 'expert', split_axis=0, concat_axis=0, tiled=True)  28.8 us
    all_to_all x1, waiting for transfers between devices, shards(): lax.all_to_all(outgoing, 'expert', split_axis=0, concat_axis=0, tiled=True)  27.6 us
    all_to_all x1, waiting for transfers between devices, shards(): lax.all_to_all(row_grad, 'expert', split_axis=0, concat_axis=0, tiled=True)  23.3 us
    psum x1, blocking collectives, shards(): lax.psum(shares[0].astype(jnp.bfloat16), 'expert').astype(jnp.float32)  21.7 us
  transfers between devices with their start and end apart: 15, of which 5 were waited for; matrix products, arithmetic and copies ran while one was open for 49% of the time, Pallas kernels for 0%

commit v1 on v0

--- a/solution.py
+++ b/solution.py
@@ -6,6 +6,17 @@
 HEADS = 8
 norm_eps = 1e-06
 highest = lax.Precision.HIGHEST
+
+
+def split_up(x, dim, size):
+    before, after = (x.shape[:dim], x.shape[dim + 1 :])
+    return jnp.moveaxis(x.reshape(*before, size, -1, *after), dim, 0)
+
+
+def laid_out(tiles, dim):
+    tiles = jnp.moveaxis(tiles, 0, dim)
+    shape = tiles.shape
+    return tiles.reshape(*shape[:dim], shape[dim] * shape[dim + 1], *shape[dim + 2 :])
 
 
 def layer_norm(matrix, norm_gain, norm_shift):
@@ -138,7 +149,14 @@
         .set(slot_rows)
         .reshape(expert_total, capacity, feature_width)
     )
-    arrived = lax.all_to_all(outgoing, "expert", split_axis=0, concat_axis=0, tiled=True)
+    length, place = (lax.axis_size("expert"), lax.axis_index("expert"))
+    blocks = split_up(outgoing, 0, length)
+    done = [blocks[place]]
+    for step in range(1, length):
+        sent = blocks[place ^ step]
+        done.append(lax.ppermute(sent, "expert", [(i, i ^ step) for i in range(length)]))
+    blocks = jnp.stack(done)[place ^ jnp.arange(length)]
+    arrived = laid_out(blocks, 0)
     flat_in = arrived.reshape(-1, feature_width)
     activation = gelu_exact(
         jnp.dot(flat_in, first_weight, preferred_element_type=jnp.float32) + first_bias

time: 726 us -> 839 us (1.16)
  waiting for transfers between devices: 136 us -> 227 us
  local copies, waits for them, and re-layouts: 138 us -> 152 us
  starting transfers between devices: 22.2 us -> 32.4 us
    ppermute x0 -> x7, waiting for transfers between devices: none -> 143 us  [shards(): lax.ppermute(sent, 'expert', [(i, i ^ step) for i in range(length)])]
    all_to_all x1 -> x0, waiting for transfers between devices: 27.6 us -> none  [shards(): lax.all_to_all(outgoing, 'expert', split_axis=0, concat_axis=0, tiled=True)]
    ppermute x0 -> x7, starting transfers between devices: none -> 13.1 us  [shards(): lax.ppermute(sent, 'expert', [(i, i ^ step) for i in range(length)])]
    psum x1, waiting for transfers between devices: 49.8 us -> 38.5 us  [shards(): lax.psum(shares[2].astype(jnp.bfloat16), 'expert').astype(jnp.float32)]
    all_to_all x1, waiting for transfers between devices: 23.3 us -> 13.5 us  [shards(): lax.all_to_all(row_grad, 'expert', split_axis=0, concat_axis=0, tiled=True)]
    unnamed x175 -> x183, local copies, waits for them, and re-layouts: 15.2 us -> 23.6 us
  transfers between devices with their start and end apart: 15 -> 21, of which waited for: 5 -> 6; matrix products, arithmetic and copies ran while one was open for 49% -> 50% of each run, Pallas kernels for 0% -> 0%
where the time goes in v1:
time: 839 us; the launch traced here: 833 us
  waiting for transfers between devices  227 us (27%)
  matrix products  201 us (24%)
  local copies, waits for them, and re-layouts  152 us (18%)
  blocking collectives  126 us (15%)
  other arithmetic  78.4 us (9%)
  starting transfers between devices  32.4 us (4%)
  between operations  15.9 us (2%)
    ppermute x7, waiting for transfers between devices, shards(): lax.ppermute(sent, 'expert', [(i, i ^ step) for i in range(length)])  143 us
    dot_general x1, matrix products, shards(): jnp.dot(flat_in, first_weight, preferred_element_type=jnp.float32)  70.8 us
    psum x1, waiting for transfers between devices, shards(): lax.psum(shares[2].astype(jnp.bfloat16), 'expert').astype(jnp.float32)  38.5 us
    pmax x1, blocking collectives, shards(): peak_logit = lax.pmax(head_peak, ('expert', 'fsdp'))  37.2 us
    dot_general x1, matrix products, shards(): jnp.einsum('rd,hd->rh', flat_grad, second_weight, preferred_element_type=...  32.2 us
    all_to_all x1, waiting for transfers between devices, shards(): lax.all_to_all(produced, 'expert', split_axis=0, concat_axis=0, tiled=True)  29.8 us
    unnamed x183, local copies, waits for them, and re-layouts  23.6 us
    psum x1, blocking collectives, shards(): lax.psum(shares[0].astype(jnp.bfloat16), 'expert').astype(jnp.float32)  20.5 us
  transfers between devices with their start and end apart: 21, of which 6 were waited for; matrix products, arithmetic and copies ran while one was open for 50% of the time, Pallas kernels for 0%

profile of v1, /device:TPU:0, one launch (start us, length us, event | category | flops | bytes accessed | tf_op | source)
XLA Modules:
  0.0 833.4 jit_solution(1059390300763560085)
XLA Ops:
  14.2 6.0 all-gather
  72.8 10.3 %all_gather.47 = bf16[512,512]{1,0:T(8,128)(2,1)} all-gather(bf16[128,512]{1,0:T(8,128)(2,1)S(1)} %copy-done.46), channel_id=1, replica_groups=mesh['expert'=8,'fsdp'=4] {'fsdp'}, dimensions={0}, use_global_device_ids=true | all-gather | bytes 655360 | tf_op jit(solution)/shard_map/all_gather | solution.py:69
  145.2 12.5 %scatter_custom_fusion = bf16[3456,512]{1,0:T(8,128)(2,1)S(1)} fusion(s32[1970]{0:T(1024)} %bitcast.169, bf16[1970,512]{1,0:T(8,128)(2,1)} %reshape.347, bf16[]{:T(256)} %constant.55.clone.1), kind=kCustom, calls=%fused_computation.70 | custom fusion | bytes 3539456 | tf_op jit(solution)/shard_map/scatter | solution.py:149
  164.2 18.4 %scatter_custom_fusion.1 = bf16[3456,512]{1,0:T(8,128)(2,1)} fusion(s32[1970]{0:T(1024)} %bitcast.170, f32[1970,512]{1,0:T(8,128)} %mul.252, f32[1970]{0:T(1024)S(1)} %mul.249, bf16[]{:T(256)} %constant.55.clone.1), kind=kCustom, calls=%fused_computation.64 | custom fusion | flops 2017280 | bytes 7594184 | tf_op jit(solution)/shard_map/scatter | solution.py:189
  199.8 86.1 %collective-permute-done.2 = bf16[1,432,512]{2,1,0:T(8,128)(2,1)S(1)} collective-permute-done((bf16[1,432,512]{2,1,0:T(8,128)(2,1)}, bf16[1,432,512]{2,1,0:T(8,128)(2,1)S(1)}, u32[]{:S(2)}, u32[]{:S(2)}) %collective-permute-start.2) | collective-permute-done | bytes 442400 | tf_op jit(solution)/shard_map/ppermute | solution.py:157
  285.9 56.8 %collective-permute-done.3 = bf16[1,432,512]{2,1,0:T(8,128)(2,1)S(1)} collective-permute-done((bf16[1,432,512]{2,1,0:T(8,128)(2,1)}, bf16[1,432,512]{2,1,0:T(8,128)(2,1)S(1)}, u32[]{:S(2)}, u32[]{:S(2)}) %collective-permute-start.3) | collective-permute-done | bytes 442400 | tf_op jit(solution)/shard_map/ppermute | solution.py:157
  345.9 70.8 %multiply_convert_fusion = (bf16[3456,2048]{1,0:T(8,128)(2,1)}, f32[3456,2048]{1,0:T(8,128)}, f32[3456,2048]{1,0:T(8,128)}) fusion(f32[2048]{0:T(1024)S(1)} %bitcast.179, bf16[3456,512]{1,0:T(8,128)(2,1)} %bitcast.149, bf16[1,512,2048]{2,1,0:T(8,128)(2,1)} %all-gather.13.cloned.1.call-done), kind=kOutput, calls=%fused_computation.8 | convolution fusion | flops 7714897920 | bytes 76423168 | tf_op jit(solution)/shard_map/dot_general | solution.py:162
  416.7 12.5 %add_convert_fusion.1 = bf16[3456,512]{1,0:T(8,128)(2,1)} fusion(bf16[3456,2048]{1,0:T(8,128)(2,1)} %get-tuple-element.48, f32[512]{0:T(512)S(1)} %bitcast.181, bf16[1,2048,512]{2,1,0:T(8,128)(2,1)} %all-gather.15.cloned.1.call-done), kind=kOutput, calls=%fused_computation.26 | convolution fusion | flops 7251296256 | bytes 19793920 | tf_op jit(solution)/shard_map/dot_general | solution.py:165
  429.2 10.3 %all-to-all-start = ((bf16[8,432,512]{2,1,0:T(8,128)(2,1)}), bf16[8,432,512]{2,1,0:T(8,128)(2,1)S(1)}, u32[]{:S(2)}, u32[]{:S(2)}) async-start(bf16[8,432,512]{2,1,0:T(8,128)(2,1)} %bitcast.152), calls=%async_computation | async-start | bytes 7077888 | tf_op jit(solution)/shard_map/all_to_all | solution.py:168
  443.0 32.2 %fusion.51 = (bf16[2048]{0:T(1024)(128)(2,1)S(1)}, bf16[3456,2048]{1,0:T(8,128)(2,1)}) fusion(f32[3456,2048]{1,0:T(8,128)} %get-tuple-element.49, bf16[3456,512]{1,0:T(8,128)(2,1)} %bitcast.43, bf16[1,2048,512]{2,1,0:T(8,128)(2,1)} %all-gather.15.cloned.1.call-done, f32[3456,2048]{1,0:T(8,128)} %get-tuple-element.65, f32[2048]{0:T(1024)S(1)} %bitcast.180), kind=kOutput, calls=%fused_computation.157 | convolution fusion | flops 7361001472 | bytes 76427264 | tf_op jit(solution)/shard_map/rd,hd->rh/dot_general | solution.py:202
  476.4 12.7 %convolution_convert_fusion = bf16[3456,512]{1,0:T(8,128)(2,1)} fusion(bf16[3456,2048]{1,0:T(8,128)(2,1)} %get-tuple-element.76, bf16[1,512,2048]{2,1,0:T(8,128)(2,1)} %all-gather.13.cloned.1.call-done), kind=kOutput, calls=%fused_computation.29 | convolution fusion | flops 7249526784 | bytes 19791872 | tf_op jit(solution)/shard_map/rh,dh->rd/dot_general | solution.py:207
  489.0 29.8 %all-to-all-done = bf16[8,432,512]{2,1,0:T(8,128)(2,1)S(1)} async-done(((bf16[8,432,512]{2,1,0:T(8,128)(2,1)}), bf16[8,432,512]{2,1,0:T(8,128)(2,1)S(1)}, u32[]{:S(2)}, u32[]{:S(2)}) %all-to-all-start) | async-done | bytes 3538976 | tf_op jit(solution)/shard_map/all_to_all | solution.py:168
  524.3 12.1 %gather_fusion.1 = bf16[1970,512]{1,0:T(8,128)(2,1)} fusion(bf16[3456,512]{1,0:T(8,128)(2,1)} %bitcast.146, s32[2048]{0:T(1024)S(1)} %copy-done.51), kind=kCustom, calls=%fused_computation.1 | custom fusion | bytes 4042440 | tf_op jit(solution)/shard_map/gather | solution.py:170
  541.8 13.8 %multiply_reduce_fusion.3 = (f32[985,2]{1,0:T(8,128)}, f32[985,512]{1,0:T(8,128)}) fusion(f32[985,2,512]{2,1,0:T(2,128)} %reshape.313, f32[985,512]{1,0:T(8,128)} %reshape.315, f32[985,2]{1,0:T(8,128)} %copy-done.23), kind=kLoop, calls=%fused_computation.32 | loop fusion | flops 3528270 | bytes 8084880 | tf_op jit(solution)/shard_map/reduce_sum | solution.py:180
  563.7 13.1 %fusion.7 = bf16[1,2048,512]{2,1,0:T(8,128)(2,1)} fusion(bf16[3456,2048]{1,0:T(8,128)(2,1)} %get-tuple-element.48, bf16[3456,512]{1,0:T(8,128)(2,1)} %bitcast.43), kind=kOutput, calls=%fused_computation.37 | convolution fusion | flops 7248805888 | bytes 19791872 | tf_op jit(solution)/shard_map/rh,rd->hd/dot_general | solution.py:200
  576.9 13.0 %fusion.8 = bf16[1,512,2048]{2,1,0:T(8,128)(2,1)} fusion(bf16[3456,512]{1,0:T(8,128)(2,1)} %bitcast.150, bf16[3456,2048]{1,0:T(8,128)(2,1)} %get-tuple-element.76), kind=kOutput, calls=%fused_computation.38 | convolution fusion | flops 7248805888 | bytes 19791872 | tf_op jit(solution)/shard_map/rd,rh->dh/dot_general | solution.py:204
  589.9 13.5 %all-to-all-done.2 = bf16[8,432,512]{2,1,0:T(8,128)(2,1)S(1)} async-done(((bf16[8,432,512]{2,1,0:T(8,128)(2,1)}), bf16[8,432,512]{2,1,0:T(8,128)(2,1)S(1)}, u32[]{:S(2)}, u32[]{:S(2)}) %all-to-all-start.2) | async-done | bytes 3538976 | tf_op jit(solution)/shard_map/all_to_all | solution.py:211
  603.5 9.3 %gather_fusion.2 = bf16[1970,512]{1,0:T(8,128)(2,1)} fusion(bf16[3456,512]{1,0:T(8,128)(2,1)S(1)} %bitcast.145, s32[2048]{0:T(1024)S(1)} %copy-done.52), kind=kCustom, calls=%fused_computation.2 | custom fusion | bytes 4042440 | tf_op jit(solution)/shard_map/gather | solution.py:213
  618.3 8.4 %reduce_sum.274 = f32[985,512]{1,0:T(8,128)} reduce(f32[985,2,512]{2,1,0:T(2,128)} %reshape.316, f32[]{:T(128)} %constant.50.clone.1), dimensions={1}, to_apply=%region_15.16 | reduce | flops 504320 | bytes 6051844 | tf_op jit(solution)/shard_map/reduce_sum | solution.py:219
  644.0 6.7 multiply_reduce_fusion.1
  704.8 37.2 %pmax.7 = f32[8]{0:T(128)S(1)} all-reduce(f32[8]{0:T(128)S(1)} %get-tuple-element.17), channel_id=1, replica_groups=mesh['expert'=8,'fsdp'=4] {'expert','fsdp'}, use_global_device_ids=true, to_apply=%region_58.59 | all-reduce | flops 8 | bytes 64 | tf_op jit(solution)/shard_map/pmax | solution.py:336
  750.6 6.4 all-reduce.10
  757.5 20.5 %all-reduce.8 = (bf16[128]{0:T(256)(128)(2,1)S(1)}, bf16[128]{0:T(256)(128)(2,1)S(1)}, bf16[128]{0:T(256)(128)(2,1)S(1)}, bf16[128]{0:T(256)(128)(2,1)S(1)}, bf1...) all-reduce(bf16[128]{0:T(256)(128)(2,1)S(1)} %dynamic-slice.1, ...), channel_id=1, replica_groups=mesh['expert'=8,'fsdp'=4] {'expert'}, use_global_device_ids=true, to_apply=%region_26.27 | all-reduce | flops 1920 | bytes 7680 | tf_op jit(solution)/shard_map/psum | solution.py:311
  784.6 38.5 %all-reduce.13.cloned.1.call-done = (bf16[128,1536]{1,0:T(8,128)(2,1)}, bf16[128,512]{1,0:T(8,128)(2,1)}) async-done(((bf16[128,1536]{1,0:T(8,128)(2,1)}, bf16[128,512]{1,0:T(8,128)(2,1)}), (bf16[128,1536]{1,0:T(8,128)(2,1)}, bf16[128,512]{1,0:T(8,128)(2,1)})) %all-reduce.13.cloned.1.call-update) | async-done | bytes 524304 | tf_op jit(solution)/shard_map/psum | solution.py:313
  (359 shorter events, 266.7 us)
Async XLA Ops:
  7.3 89.3 %all-gather.11.cloned.1.call-start = ((), (), s32[]{:S(2)}) async-start(), calls=%async_computation.10 | async-start | bytes 1966080 | tf_op jit(solution)/shard_map/all_gather | solution.py:66
  8.1 337.8 %all-gather.13.cloned.1.call-start = ((), (), s32[]{:S(2)}) async-start(), calls=%async_computation.11 | async-start | bytes 2621440 | tf_op jit(solution)/shard_map/all_gather | solution.py:74
  8.8 407.9 %all-gather.15.cloned.1.call-start = ((), (), s32[]{:S(2)}) async-start(), calls=%async_computation.12 | async-start | bytes 2621440 | tf_op jit(solution)/shard_map/all_gather | solution.py:76
  14.2 122.4 %copy-start.5 = (f32[985,512]{1,0:T(8,128)}, f32[985,512]{1,0:T(8,128)S(1)}, u32[]{:S(2)}) copy-start(f32[985,512]{1,0:T(8,128)S(1)} %reshape.287) | copy-start | bytes 6051844
  45.7 94.0 %copy-start.53 = (f32[4,1,128]{2,1,0:T(1,128)}, f32[4,1,128]{2,1,0:T(1,128)S(1)}, u32[]{:S(2)}) copy-start(f32[4,1,128]{2,1,0:T(1,128)S(1)} %convert_element_type.339) | copy-start | bytes 6148
  50.7 89.0 %copy-start.62 = (f32[4,1,128]{2,1,0:T(1,128)}, f32[4,1,128]{2,1,0:T(1,128)S(1)}, u32[]{:S(2)}) copy-start(f32[4,1,128]{2,1,0:T(1,128)S(1)} %convert_element_type.340) | copy-start | bytes 6148
  159.5 39.2 %collective-permute-start.1 = (bf16[1,432,512]{2,1,0:T(8,128)(2,1)}, bf16[1,432,512]{2,1,0:T(8,128)(2,1)}, u32[]{:S(2)}, u32[]{:S(2)}) collective-permute-start(bf16[1,432,512]{2,1,0:T(8,128)(2,1)} %get-tuple-element.57), channel_id=1, source_target_pairs={{0,8},{4,12},{8,0},{12,4},{16,24},{20,28},{24,16},{28,20},{1,9},{5... | collective-permute-start | bytes 1327112 | tf_op jit(solution)/shard_map/ppermute | solution.py:157
  161.0 32.5 %collective-permute-start = (bf16[1,432,512]{2,1,0:T(8,128)(2,1)}, bf16[1,432,512]{2,1,0:T(8,128)(2,1)}, u32[]{:S(2)}, u32[]{:S(2)}) collective-permute-start(bf16[1,432,512]{2,1,0:T(8,128)(2,1)} %get-tuple-element.58), channel_id=1, source_target_pairs={{0,4},{4,0},{8,12},{12,8},{16,20},{20,16},{24,28},{28,24},{1,5},{5... | collective-permute-start | bytes 1327112 | tf_op jit(solution)/shard_map/ppermute | solution.py:157
  182.7 246.5 %all-to-all-start.1 = ((bf16[8,432,512]{2,1,0:T(8,128)(2,1)}), bf16[8,432,512]{2,1,0:T(8,128)(2,1)}, u32[]{:S(2)}, u32[]{:S(2)}) async-start(bf16[8,432,512]{2,1,0:T(8,128)(2,1)} %bitcast.42), calls=%async_computation.1 | async-start | bytes 7077888 | tf_op jit(solution)/shard_map/all_to_all | solution.py:192
  187.6 155.7 %collective-permute-start.6 = (bf16[1,432,512]{2,1,0:T(8,128)(2,1)}, bf16[1,432,512]{2,1,0:T(8,128)(2,1)S(1)}, u32[]{:S(2)}, u32[]{:S(2)}) collective-permute-start(bf16[1,432,512]{2,1,0:T(8,128)(2,1)} %get-tuple-element.52), channel_id=1, source_target_pairs={{0,28},{4,24},{8,20},{12,16},{16,12},{20,8},{24,4},{28,0},{1,29},{... | collective-permute-start | bytes 1327112 | tf_op jit(solution)/shard_map/ppermute | solution.py:157
  192.4 150.9 %collective-permute-start.5 = (bf16[1,432,512]{2,1,0:T(8,128)(2,1)}, bf16[1,432,512]{2,1,0:T(8,128)(2,1)S(1)}, u32[]{:S(2)}, u32[]{:S(2)}) collective-permute-start(bf16[1,432,512]{2,1,0:T(8,128)(2,1)} %get-tuple-element.53), channel_id=1, source_target_pairs={{0,24},{4,28},{8,16},{12,20},{16,8},{20,12},{24,0},{28,4},{1,25},{... | collective-permute-start | bytes 1327112 | tf_op jit(solution)/shard_map/ppermute | solution.py:157
  192.9 150.3 %collective-permute-start.4 = (bf16[1,432,512]{2,1,0:T(8,128)(2,1)}, bf16[1,432,512]{2,1,0:T(8,128)(2,1)S(1)}, u32[]{:S(2)}, u32[]{:S(2)}) collective-permute-start(bf16[1,432,512]{2,1,0:T(8,128)(2,1)} %get-tuple-element.54), channel_id=1, source_target_pairs={{0,20},{4,16},{8,28},{12,24},{16,4},{20,0},{24,12},{28,8},{1,21},{... | collective-permute-start | bytes 1327112 | tf_op jit(solution)/shard_map/ppermute | solution.py:157
  193.5 92.4 %collective-permute-start.2 = (bf16[1,432,512]{2,1,0:T(8,128)(2,1)}, bf16[1,432,512]{2,1,0:T(8,128)(2,1)S(1)}, u32[]{:S(2)}, u32[]{:S(2)}) collective-permute-start(bf16[1,432,512]{2,1,0:T(8,128)(2,1)} %get-tuple-element.56), channel_id=1, source_target_pairs={{0,12},{4,8},{8,4},{12,0},{16,28},{20,24},{24,20},{28,16},{1,13},{... | collective-permute-start | bytes 1327112 | tf_op jit(solution)/shard_map/ppermute | solution.py:157
  198.7 144.0 %collective-permute-start.3 = (bf16[1,432,512]{2,1,0:T(8,128)(2,1)}, bf16[1,432,512]{2,1,0:T(8,128)(2,1)S(1)}, u32[]{:S(2)}, u32[]{:S(2)}) collective-permute-start(bf16[1,432,512]{2,1,0:T(8,128)(2,1)} %get-tuple-element.55), channel_id=1, source_target_pairs={{0,16},{4,20},{8,24},{12,28},{16,0},{20,4},{24,8},{28,12},{1,17},{... | collective-permute-start | bytes 1327112 | tf_op jit(solution)/shard_map/ppermute | solution.py:157
  429.2 89.6 %all-to-all-start = ((bf16[8,432,512]{2,1,0:T(8,128)(2,1)}), bf16[8,432,512]{2,1,0:T(8,128)(2,1)S(1)}, u32[]{:S(2)}, u32[]{:S(2)}) async-start(bf16[8,432,512]{2,1,0:T(8,128)(2,1)} %bitcast.152), calls=%async_computation | async-start | bytes 7077888 | tf_op jit(solution)/shard_map/all_to_all | solution.py:168
  439.5 257.1 %reduce-scatter.26.cloned.1.call-start = ((), (), s32[]{:S(2)}) async-start(), calls=%async_computation.19 | async-start | bytes 163840
  442.9 255.0 %reduce-scatter.24.cloned.1.call-start = ((), (), s32[]{:S(2)}) async-start(), calls=%async_computation.18 | async-start | bytes 655360
  520.5 83.0 %all-to-all-start.2 = ((bf16[8,432,512]{2,1,0:T(8,128)(2,1)}), bf16[8,432,512]{2,1,0:T(8,128)(2,1)S(1)}, u32[]{:S(2)}, u32[]{:S(2)}) async-start(bf16[8,432,512]{2,1,0:T(8,128)(2,1)} %bitcast.151), calls=%async_computation.2 | async-start | bytes 7077888 | tf_op jit(solution)/shard_map/all_to_all | solution.py:211
  524.2 175.4 %reduce-scatter.22.cloned.1.call-start = ((), (), s32[]{:S(2)}) async-start(), calls=%async_computation.17 | async-start | bytes 163840
  563.6 136.8 %reduce-scatter.20.cloned.1.call-start = ((), (), s32[]{:S(2)}) async-start(), calls=%async_computation.16 | async-start | bytes 2621440 | tf_op jit(solution)/shard_map/reduce_scatter | solution.py:329
  576.8 125.8 %reduce-scatter.18.cloned.1.call-start = ((), (), s32[]{:S(2)}) async-start(), calls=%async_computation.15 | async-start | bytes 2621440 | tf_op jit(solution)/shard_map/reduce_scatter | solution.py:323
  589.9 159.2 %reduce-scatter.16.cloned.1.call-start = ((), (), s32[]{:S(2)}) async-start(), calls=%async_computation.14 | async-start | bytes 655360 | tf_op jit(solution)/shard_map/reduce_scatter | solution.py:294
  662.9 86.2 %reduce-scatter.14.cloned.1.call-start = ((), (), s32[]{:S(2)}) async-start(), calls=%async_computation.13 | async-start | bytes 1966080 | tf_op jit(solution)/shard_map/reduce_scatter | solution.py:285
  695.3 127.8 %all-reduce.13.cloned.1.call-start = ((), (), s32[]{:S(2)}) async-start(), calls=%async_computation.20 | async-start | bytes 1048576 | tf_op jit(solution)/shard_map/psum | solution.py:313
  (76 other events, 1276.8 us)
Sparse Core Ops, SparseCore 0:
  9.7 22.3 all-gather.10
  33.7 22.6 all-gather.12
  57.9 24.9 all-gather.14
  443.1 20.0 reduce-scatter.25
  476.5 22.0 reduce-scatter.23
  563.8 19.9 reduce-scatter.21
  586.5 31.3 reduce-scatter.19
  620.4 31.4 reduce-scatter.17
  663.0 19.4 reduce-scatter.15
  695.4 26.2 reduce-scatter.13
  749.3 73.7 all-reduce.12
